TPU v7x, 32 devices: a whole 2x2x4 slice. The times are simulated.
32 devices in a mesh: chan: 4 (over y, core), tile: 8 (over z, x).
Axes of the slice: x: 2, y: 2, z: 4, core: 2. Of those that a mesh axis runs over, the one named last changes fastest.
Arguments:
- dirty: float32 [2, 36, 128, 128], P(None, 'chan', 'tile'), may hold values from -6 to 6
- beams: float32 [36, 289], P('chan'), may hold values from -0.24 to 0.24
- chan_bins: int32 [36], replicated, may hold values from 0 to 287
- pixel_order: int32 [8, 2048], P('tile'), may hold values from 0 to 2047, each once within a row
Outputs:
- spectrum: float32 [2, 256, 8, 2048], P(None, None, 'tile', 'chan')
- residual: float32 [2, 36, 128, 128], P(None, 'chan', 'tile')
Inputs may be any that keep to these rules, and one draw needn't show every extreme that they name: `pixel_order`: each row is a permutation of 0 to 2047.
All inputs are finite; a program needn't handle non-finite values.
Results may differ from a plain program's by a relative error of at most 0.000068.
Values sent between devices are 32-bit elements; how exact they have to be, the bound alone decides.
A program may use at most 64 MiB of HBM per device.

v0:
```python
import math

import jax
import jax.numpy as jnp
from jax import lax
from jax.sharding import PartitionSpec as P

DEPTHS = 256
BINS = 288


THRESHOLD = 0.8
STEP_SIZE = 0.5
HIGH = lax.Precision.HIGHEST


def with_halo(cells, sides, width):
    for axis, dim in sides:
        count = lax.axis_size(axis)
        ends = count - 1
        head = lax.slice_in_dim(cells, 0, width, axis=dim)
        tail = lax.slice_in_dim(cells, cells.shape[dim] - width, cells.shape[dim], axis=dim)
        cells = jnp.concatenate(
            [
                lax.ppermute(tail, axis, [(i, (i + 1) % count) for i in range(ends)]),
                cells,
                lax.ppermute(head, axis, [((i + 1) % count, i) for i in range(ends)]),
            ],
            axis=dim,
        )
    return cells


def analysis_matrix(bin_list, channels):
    depth_index = jnp.arange(DEPTHS, dtype=jnp.int32) - DEPTHS // 2
    turn_count = jnp.mod(bin_list[:, None] * depth_index[None, :], BINS)
    angles = turn_count.astype(jnp.float32) * (2.0 * math.pi / BINS)
    cosine = jnp.cos(angles).T
    sine_part = jnp.sin(angles).T
    upper = jnp.concatenate([cosine, sine_part], axis=1)
    lower = jnp.concatenate([-sine_part, cosine], axis=1)
    return jnp.concatenate([upper, lower], axis=0) * (1.0 / math.sqrt(channels))


def shrink(spectra):
    depth_count = spectra.shape[0] // 2
    real_part = spectra[:depth_count]
    imag_part = spectra[depth_count:]
    magnitude = jnp.sqrt(real_part * real_part + imag_part * imag_part)
    factor = jnp.maximum(magnitude - THRESHOLD, 0.0) / jnp.maximum(magnitude, THRESHOLD)
    return spectra * jnp.concatenate([factor, factor], axis=0)


def blur(field, beams, row_pad):
    pair_count, chan_count, row_count, col_count = field.shape
    beam_width = math.isqrt(beams.shape[1])
    beam_edge = (beam_width - 1) // 2
    kernel = beams.reshape(chan_count, beam_width, beam_width)
    kernel = jnp.concatenate([kernel, kernel], axis=0)[:, None]
    stacked = field.reshape(1, pair_count * chan_count, row_count, col_count)
    blurred = lax.conv_general_dilated(
        stacked,
        kernel,
        (1, 1),
        ((row_pad, row_pad), (beam_edge, beam_edge)),
        feature_group_count=pair_count * chan_count,
        precision=HIGH,
    )
    return blurred.reshape(pair_count, chan_count, blurred.shape[2], col_count)


def on_device(dirty, beams, chan_bins, pixel_order):
    pair_count, chan_local, row_count, col_count = dirty.shape
    channels = chan_bins.shape[0]
    groups = lax.axis_size("chan")
    tile_pix = row_count * col_count
    owned = tile_pix // groups
    beam_edge = (math.isqrt(beams.shape[1]) - 1) // 2
    analysis = analysis_matrix(chan_bins, channels)
    slot_pixels = pixel_order[0]
    inverse = (
        jnp.zeros((tile_pix,), jnp.int32).at[slot_pixels].set(jnp.arange(tile_pix, dtype=jnp.int32))
    )

    def project(cube_block):
        flattened = cube_block.reshape(pair_count * channels, cube_block.shape[3])
        return jnp.dot(analysis, flattened, precision=HIGH, preferred_element_type=jnp.float32)

    def to_owners(cube):
        slots = jnp.take(cube.reshape(pair_count, chan_local, tile_pix), slot_pixels, axis=2)
        slots = slots.reshape(pair_count, chan_local, groups, owned)
        return project(lax.all_to_all(slots, "chan", split_axis=2, concat_axis=1, tiled=True))

    first = shrink(to_owners(dirty))
    owner_model = jnp.dot(analysis.T, first, precision=HIGH, preferred_element_type=jnp.float32)
    owner_model = owner_model.reshape(pair_count, channels, 1, owned)
    model_slots = lax.all_to_all(owner_model, "chan", split_axis=1, concat_axis=2, tiled=True)
    model = jnp.take(model_slots.reshape(pair_count, chan_local, tile_pix), inverse, axis=2)
    model = model.reshape(dirty.shape)
    padded = with_halo(model, (("tile", 2),), beam_edge)
    residual = dirty - blur(padded, beams, 0)
    second = shrink(first + STEP_SIZE * to_owners(residual))
    return (second.reshape(pair_count, DEPTHS, 1, owned), residual)


def solution(mesh):
    placed = (P(None, "chan", "tile", None), P("chan", None), P(), P("tile", None))
    return jax.shard_map(
        on_device,
        mesh=mesh,
        in_specs=placed,
        out_specs=(P(None, None, "tile", "chan"), P(None, "chan", "tile", None)),
        check_vma=False,
    )
```

profile of v0, /device:TPU:0, one launch (start us, length us, event | category | flops | bytes accessed | tf_op | source)
XLA Modules:
  0.0 190.5 jit_solution(454370934873426785)
XLA Ops:
  0.6 0.7 fusion.24
  1.3 0.7 compare_and_fusion.1
  2.0 1.8 copy.61
  3.9 14.5 %gather_fusion = f32[2048,2,9]{2,1,0:T(2,128)} fusion(f32[2,9,2048]{1,0,2:T(2,128)S(1)} %bitcast.65, s32[2048]{0:T(1024)S(1)} %fusion.24), kind=kCustom, calls=%fused_computation.clone | custom fusion | bytes 303104 | tf_op jit(solution)/shard_map/jit(_take)/gather | solution.py:90
  18.3 10.0 %broadcast_select_fusion.2 = f32[2048,2,9]{2,1,0:T(2,128)S(1)} fusion(f32[2048,2,9]{2,1,0:T(2,128)} %gather_fusion, pred[2048]{0:T(1024)(128)(4,1)S(1)} %compare_and_fusion.1), kind=kLoop, calls=%fused_computation.14 | loop fusion | flops 36864 | bytes 296960 | tf_op jit(solution)/shard_map/jit(_take)/select_n | solution.py:90
  28.3 0.0 copy-start.7
  28.3 0.0 copy-start.9
  28.3 0.0 copy-start.8
  28.3 1.9 %copy.32 = f32[2,9,4,512]{3,0,1,2:T(2,128)} copy(f32[2,9,4,512]{1,0,3,2:T(2,128)S(1)} %bitcast.60) | data formatting | bytes 294912 | tf_op jit(solution)/shard_map/reshape | solution.py:91
  30.3 4.3 %all-to-all-start = ((f32[2,9,4,512]{3,0,1,2:T(2,128)}), f32[2,9,4,512]{3,0,1,2:T(2,128)S(1)}, u32[]{:S(2)}, u32[]{:S(2)}) async-start(f32[2,9,4,512]{3,0,1,2:T(2,128)} %copy.32), calls=%async_computation | async-start | bytes 294912 | tf_op jit(solution)/shard_map/all_to_all | solution.py:92
  34.5 0.0 copy-done.7
  34.6 8.0 %scatter_custom_fusion = s32[2048]{0:T(1024)S(1)} fusion(s32[2048]{0:T(1024)S(1)} %bitcast.74, s32[2048]{0:T(1024)S(1)} %iota.9, s32[]{:T(128)} %constant.20.clone.1), kind=kCustom, calls=%fused_computation.51 | custom fusion | bytes 8196 | tf_op jit(solution)/shard_map/scatter | solution.py:82
  42.6 0.0 copy-done.9
  42.6 0.6 fusion.20
  43.3 0.0 copy-start.1
  43.3 0.0 copy-start.3
  43.3 0.0 copy-done.8
  43.3 0.1 reshape.92
  43.4 0.2 copy.43
  43.6 0.0 all-to-all-done
  43.7 1.0 fusion.32
  44.8 0.3 maximum_divide_fusion.1
  45.0 0.0 copy-done.1
  45.1 0.8 copy-done
  45.9 0.8 fusion.11
  46.7 0.8 copy.34
  47.5 3.4 %all-to-all-start.1 = ((f32[2,36,1,512]{3,0,2,1:T(2,128)}), f32[2,36,1,512]{3,0,2,1:T(2,128)S(1)}, u32[]{:S(2)}, u32[]{:S(2)}) async-start(f32[2,36,1,512]{3,0,2,1:T(2,128)} %copy.34), calls=%async_computation.1 | async-start | bytes 294912 | tf_op jit(solution)/shard_map/all_to_all | solution.py:97
  50.9 0.1 pad_maximum_fusion
  51.0 0.8 broadcast_in_dim.15
  51.8 3.9 %all-to-all-done.1 = f32[2,36,1,512]{3,0,2,1:T(2,128)S(1)} async-done(((f32[2,36,1,512]{3,0,2,1:T(2,128)}), f32[2,36,1,512]{3,0,2,1:T(2,128)S(1)}, u32[]{:S(2)}, u32[]{:S(2)}) %all-to-all-start.1) | async-done | bytes 147488 | tf_op jit(solution)/shard_map/all_to_all | solution.py:97
  55.6 2.3 %copy.56 = f32[2,9,4,1,512]{1,0,4,2,3:T(2,128)} copy(f32[2,9,4,1,512]{4,0,1,2,3:T(2,128)S(1)} %bitcast.66) | data formatting | bytes 294912 | tf_op jit(solution)/shard_map/reshape | solution.py:98
  57.9 8.4 %gather_fusion.1 = f32[2048,2,9]{2,1,0:T(2,128)S(1)} fusion(f32[2,9,2048]{1,0,2:T(2,128)} %bitcast.63, s32[2048]{0:T(1024)S(1)} %fusion.25), kind=kCustom, calls=%fused_computation.1.clone | custom fusion | bytes 303104 | tf_op jit(solution)/shard_map/jit(_take)/gather | solution.py:98
  66.3 7.4 %broadcast_select_fusion = f32[2048,2,9]{2,1,0:T(2,128)S(1)} fusion(f32[2048,2,9]{2,1,0:T(2,128)S(1)} %gather_fusion.1, pred[2048]{0:T(1024)(128)(4,1)S(1)} %compare_and_fusion), kind=kLoop, calls=%fused_computation.12 | loop fusion | flops 36864 | bytes 296960 | tf_op jit(solution)/shard_map/jit(_take)/select_n | solution.py:98
  73.8 1.5 fusion.33
  75.3 1.6 copy.64
  76.8 3.9 %collective-permute-start = (f32[2,9,8,128]{3,2,1,0:T(8,128)S(1)}, f32[2,9,8,128]{3,2,1,0:T(8,128)S(1)}, u32[]{:S(2)}, u32[]{:S(2)}) collective-permute-start(f32[2,9,8,128]{3,2,1,0:T(8,128)S(1)} %copy.64), channel_id=1, source_target_pairs={{0,1},{1,2},{2,3},{3,4},{4,5},{5,6},{6,7},{8,9},{9,10},{10,11},{11... | collective-permute-start | bytes 221192 | tf_op jit(solution)/shard_map/ppermute | solution.py:25
  80.8 2.2 %copy.65 = f32[2,9,8,128]{3,2,1,0:T(8,128)} copy(f32[2,9,8,128]{1,0,3,2:T(2,128)} %get-tuple-element.10) | data formatting | bytes 147456
  82.9 1.5 collective-permute-start.1
  84.4 8.3 %fusion.37 = f32[2,9,2048]{1,0,2:T(2,128)} fusion(f32[2048,2,9]{2,1,0:T(2,128)S(1)} %gather_fusion.1, pred[2048]{0:T(1024)(128)(4,1)S(1)} %compare_and_fusion), kind=kLoop, calls=%fused_computation.60 | loop fusion | flops 36864 | bytes 296960 | tf_op jit(solution)/shard_map/jit(_take)/select_n | solution.py:98
  92.7 2.7 %copy.38 = f32[2,9,2048]{2,1,0:T(8,128)S(1)} copy(f32[2,9,2048]{1,0,2:T(2,128)} %fusion.37) | data formatting | bytes 294912 | tf_op jit(solution)/shard_map/jit(_take)/select_n | solution.py:98
  95.5 0.0 collective-permute-done
  95.5 0.0 collective-permute-done.1
  95.5 1.5 copy.66
  97.0 2.0 %pad.clone = f32[18,32,1,144]{1,2,3,0:T(1,128)} pad(f32[18,32,1,128]{1,2,3,0:T(1,128)S(1)} %copy.66, f32[]{:T(128)} %constant.39.clone.1), padding=0_0x0_0x0_0x8_8 | pad | bytes 626692 | tf_op jit(solution)/shard_map/concatenate | solution.py:23
  99.0 4.4 %copy.42 = f32[18,32,1,8,18]{0,3,4,1,2:T(8,128)S(1)} copy(f32[18,32,1,8,18]{1,2,4,3,0:T(1,128)} %bitcast.61) | data formatting | bytes 663552 | tf_op jit(solution)/shard_map/conv_general_dilated | solution.py:61
  103.5 0.3 slice.36
  103.7 0.0 copy-start.10
  103.8 0.3 fusion.41
  104.1 0.5 copy-done.6
  104.6 0.0 copy-done.10
  104.7 42.8 %fusion.8 = f32[16,8,18,18]{3,1,2,0:T(8,128)S(1)} fusion(f32[18,1,17,17]{0,1,3,2:T(1,128)S(1)} %copy-done.6, pred[8,18]{0,1:T(8,128)(4,1)S(1)} %copy-done.10, f32[18,32,8,34]{0,2,3,1:T(8,128)S(1)} %fusion.41), kind=kOutput, calls=%fused_computation.17 | convolution fusion | flops 143866368 | bytes 813528 | tf_op jit(solution)/shard_map/conv_general_dilated | solution.py:61
  147.4 1.3 copy.45
  148.8 0.3 reshape.104
  149.2 0.9 sub.15
  150.1 0.0 copy-start.5
  150.1 1.0 copy.63
  151.1 14.5 %gather_fusion.2 = f32[2048,2,9]{2,1,0:T(2,128)} fusion(f32[2,9,2048]{1,0,2:T(2,128)S(1)} %bitcast.64, s32[2048]{0:T(1024)S(1)} %fusion.24), kind=kCustom, calls=%fused_computation.2.clone | custom fusion | bytes 303104 | tf_op jit(solution)/shard_map/jit(_take)/gather | solution.py:90
  165.5 10.0 %broadcast_select_fusion.1 = f32[2048,2,9]{2,1,0:T(2,128)S(1)} fusion(f32[2048,2,9]{2,1,0:T(2,128)} %gather_fusion.2, pred[2048]{0:T(1024)(128)(4,1)S(1)} %compare_and_fusion.1), kind=kLoop, calls=%fused_computation.13 | loop fusion | flops 36864 | bytes 296960 | tf_op jit(solution)/shard_map/jit(_take)/select_n | solution.py:90
  175.5 1.9 %copy.49 = f32[2,9,4,512]{3,0,1,2:T(2,128)} copy(f32[2,9,4,512]{1,0,3,2:T(2,128)S(1)} %bitcast.59) | data formatting | bytes 294912 | tf_op jit(solution)/shard_map/reshape | solution.py:91
  177.5 8.1 %all_to_all.45 = f32[2,9,4,512]{3,0,1,2:T(2,128)S(1)} all-to-all(f32[2,9,4,512]{3,0,1,2:T(2,128)} %copy.49), channel_id=1, replica_groups=mesh['chan'=4,'tile'=8] {'chan'}, dimensions={2} | all-to-all | bytes 294912 | tf_op jit(solution)/shard_map/all_to_all | solution.py:92
  185.7 2.3 %fusion.7 = f32[512,512]{1,0:T(8,128)S(1)} fusion(f32[72,512]{1,0:T(8,128)S(1)} %reshape.96, f32[512,512]{1,0:T(8,128)S(1)} %fusion.32, f32[256,512]{1,0:T(8,128)} %copy-done, f32[256,36]{1,0:T(8,128)S(1)} %copy-done.4, f32[256,36]{1,0:T(8,128)S(1)} %copy-done.2, f32[256,36]{1,0:T(8,128)S(1)} %get-tuple-element.11), kind=kOutput, calls=%fused_computation.16 | convolution fusion | flops 227688448 | bytes 2879488 | tf_op jit(solution)/shard_map/dot_general | solution.py:87
  188.0 0.3 maximum_divide_fusion
  188.3 0.2 maximum_multiply_fusion.1
  188.4 2.0 %copy.51 = f32[2,256,1,512]{3,2,1,0:T(1,128)} copy(f32[2,256,1,512]{3,1,0,2:T(8,128)S(1)} %bitcast.62) | data formatting | bytes 2097152
  (21 shorter events, 0.3 us)
Async XLA Ops:
  28.3 6.2 %copy-start.7 = (s32[1,2048]{1,0:T(1,128)S(1)}, s32[1,2048]{1,0:T(1,128)}, u32[]{:S(2)}) copy-start(s32[1,2048]{1,0:T(1,128)} %param.9) | copy-start | bytes 24580
  28.3 14.3 %copy-start.9 = (s32[36]{0:T(128)S(1)}, s32[36]{0:T(128)}, u32[]{:S(2)}) copy-start(s32[36]{0:T(128)} %param.8) | copy-start | bytes 436
  28.3 15.0 %copy-start.8 = (f32[9,289]{1,0:T(8,128)S(1)}, f32[9,289]{1,0:T(8,128)}, u32[]{:S(2)}) copy-start(f32[9,289]{1,0:T(8,128)} %param.7) | copy-start | bytes 31216
  30.3 13.4 %all-to-all-start = ((f32[2,9,4,512]{3,0,1,2:T(2,128)}), f32[2,9,4,512]{3,0,1,2:T(2,128)S(1)}, u32[]{:S(2)}, u32[]{:S(2)}) async-start(f32[2,9,4,512]{3,0,1,2:T(2,128)} %copy.32), calls=%async_computation | async-start | bytes 294912 | tf_op jit(solution)/shard_map/all_to_all | solution.py:92
  43.3 1.8 copy-start.1
  43.3 1.8 copy-start.3
  45.1 0.8 copy-start
  47.5 8.1 %all-to-all-start.1 = ((f32[2,36,1,512]{3,0,2,1:T(2,128)}), f32[2,36,1,512]{3,0,2,1:T(2,128)S(1)}, u32[]{:S(2)}, u32[]{:S(2)}) async-start(f32[2,36,1,512]{3,0,2,1:T(2,128)} %copy.34), calls=%async_computation.1 | async-start | bytes 294912 | tf_op jit(solution)/shard_map/all_to_all | solution.py:97
  76.8 18.7 %collective-permute-start = (f32[2,9,8,128]{3,2,1,0:T(8,128)S(1)}, f32[2,9,8,128]{3,2,1,0:T(8,128)S(1)}, u32[]{:S(2)}, u32[]{:S(2)}) collective-permute-start(f32[2,9,8,128]{3,2,1,0:T(8,128)S(1)} %copy.64), channel_id=1, source_target_pairs={{0,1},{1,2},{2,3},{3,4},{4,5},{5,6},{6,7},{8,9},{9,10},{10,11},{11... | collective-permute-start | bytes 221192 | tf_op jit(solution)/shard_map/ppermute | solution.py:25
  82.9 12.5 %collective-permute-start.1 = (f32[2,9,8,128]{3,2,1,0:T(8,128)}, f32[2,9,8,128]{3,2,1,0:T(8,128)S(1)}, u32[]{:S(2)}, u32[]{:S(2)}) collective-permute-start(f32[2,9,8,128]{3,2,1,0:T(8,128)} %copy.65), channel_id=1, source_target_pairs={{1,0},{2,1},{3,2},{4,3},{5,4},{6,5},{7,6},{9,8},{10,9},{11,10},{12... | collective-permute-start | bytes 221192 | tf_op jit(solution)/shard_map/ppermute | solution.py:27
  103.7 0.9 copy-start.6
  103.7 0.9 copy-start.10
  150.1 15.5 %copy-start.5 = (f32[2,9,16,128]{3,2,1,0:T(8,128)}, f32[2,9,16,128]{3,2,1,0:T(8,128)S(1)}, u32[]{:S(2)}) copy-start(f32[2,9,16,128]{3,2,1,0:T(8,128)S(1)} %sub.15) | copy-start | bytes 442372
  175.5 10.1 %copy-start.2 = (f32[256,36]{1,0:T(8,128)S(1)}, f32[256,36]{1,0:T(8,128)}, u32[]{:S(2)}) copy-start(f32[256,36]{1,0:T(8,128)} %copy-done.1) | copy-start | bytes 110596
  175.5 10.1 %copy-start.4 = (f32[256,36]{1,0:T(8,128)S(1)}, f32[256,36]{1,0:T(8,128)}, u32[]{:S(2)}) copy-start(f32[256,36]{1,0:T(8,128)} %copy-done.3) | copy-start | bytes 110596
where the time goes:
time: 192 us; the launch traced here: 190 us
  local copies, waits for them, and re-layouts  77.6 us (40%)
  matrix products  47 us (24%)
  other arithmetic  39.9 us (21%)
  starting transfers between devices  13 us (7%)
  blocking collectives  8.08 us (4%)
  waiting for transfers between devices  3.89 us (2%)
    conv_general_dilated x1, matrix products, blur(): lax.conv_general_dilated(stacked, kernel, (1, 1), ((row_pad, row_pad), (b...  42.8 us
    gather x2, local copies, waits for them, and re-layouts, to_owners(): jnp.take(cube.reshape(pair_count, chan_local, tile_pix), slot_pixels, axi...  28.9 us
    select_n x2, other arithmetic, to_owners(): jnp.take(cube.reshape(pair_count, chan_local, tile_pix), slot_pixels, axi...  19.9 us
    select_n x2, other arithmetic, on_device(): jnp.take(model_slots.reshape(pair_count, chan_local, tile_pix), inverse,...  15.8 us
    unnamed x26, local copies, waits for them, and re-layouts  8.69 us
    gather x1, local copies, waits for them, and re-layouts, on_device(): jnp.take(model_slots.reshape(pair_count, chan_local, tile_pix), inverse,...  8.39 us
    all_to_all x1, blocking collectives, to_owners(): lax.all_to_all(slots, 'chan', split_axis=2, concat_axis=1, tiled=True)  8.08 us
    scatter x1, local copies, waits for them, and re-layouts, on_device(): jnp.zeros((tile_pix,), jnp.int32).at[slot_pixels]  8.05 us
  transfers between devices with their start and end apart: 4, of which 1 were waited for; matrix products, arithmetic and copies ran while one was open for 12% of the time, Pallas kernels for 0%

commit v1 on v0

v1 whole, which is shorter than its diff:
```python
import functools
import math

import jax
import jax.numpy as jnp
from jax import lax
from jax.experimental import pallas as pl
from jax.experimental.pallas import tpu as pltpu
from jax.sharding import PartitionSpec as P

DEPTHS = 256
BINS = 288
THRESHOLD = 0.8
STEP_SIZE = 0.5
MESH = pl.DeviceIdType.MESH
LANES = 128
F32 = jnp.float32
BF16 = jnp.bfloat16


def round_up(value, unit):
    return (value + unit - 1) // unit * unit


def split(x):
    high = x.astype(BF16)
    return high, (x - high.astype(F32)).astype(BF16)


def shrink_pair(a, b):
    squared = a * a + b * b
    factor = jnp.maximum(1.0 - THRESHOLD * lax.rsqrt(jnp.maximum(squared, 1e-30)), 0.0)
    return a * factor, b * factor


def mxu(a, b):
    return jnp.dot(a, b, preferred_element_type=F32)


def kernel(
    d,
    dirty,
    beams,
    bins,
    order,
    out,
    res,
    bincol,
    at3,
    a3,
    at2,
    x,
    big,
    first_hi,
    first_lo,
    first_slots,
    model,
    padded,
    slots,
    mixed,
    send_a,
    send_d,
    send_m,
    send_r,
    recv_a,
    recv_d,
    recv_m,
    recv_h,
    recv_r,
    sems_a,
    sems_d,
    sems_m,
    sems_h,
    sems_r,
):
    G, T, R, Y, C, S, W, CC, NCH, HALF, BEAM = (
        d["G"], d["T"], d["R"], d["Y"], d["C"], d["S"], d["W"], d["CC"], d["NCH"], d["HALF"], d["BEAM"]
    )
    SC = S * C
    KP = d["KP"]
    g = lax.axis_index("chan")
    t = lax.axis_index("tile")
    has_prev = t > 0
    has_next = t < T - 1
    before = lax.rem(t + T - 1, T)
    after = lax.rem(t + 1, T)

    barrier = pltpu.get_barrier_semaphore()
    for step in range(1, G):
        pl.semaphore_signal(barrier, inc=1, device_id=(lax.rem(g + step, G), t), device_id_type=MESH)

    @pl.when(has_prev)
    def _():
        for p in range(G):
            pl.semaphore_signal(barrier, inc=1, device_id=(p, before), device_id_type=MESH)

    @pl.when(has_next)
    def _():
        for p in range(G):
            pl.semaphore_signal(barrier, inc=1, device_id=(p, after), device_id_type=MESH)

    def pack(send, k, cells):
        for p in range(G):
            for r in range(R):
                send[p, k, r * W : r * W + W, :] = cells[pl.ds(k * W * Y + p * R + r, W, stride=Y), :]

    for c in range(C):
        for s in range(S):
            mixed[(c * S + s) * Y : (c * S + s) * Y + Y, :] = dirty[(s * C + c) * Y : (s * C + c) * Y + Y, :]
    for k in range(NCH):
        pack(send_a, k, mixed)
    near = has_prev.astype(jnp.int32) + has_next.astype(jnp.int32)
    pl.semaphore_wait(barrier, G - 1 + G * near)

    def own_copies(src, dst, sems, *k):
        out_copies, in_copies = [], []
        for step in range(1, G):
            p = lax.rem(g + step, G)
            out_copies.append(
                pltpu.make_async_remote_copy(
                    src(p), dst(g), sems.at[(0, p, *k)], sems.at[(1, g, *k)], device_id=(p, t), device_id_type=MESH
                )
            )
            in_copies.append(
                pltpu.make_async_remote_copy(
                    src(p), dst(p), sems.at[(0, p, *k)], sems.at[(1, p, *k)], device_id=(p, t), device_id_type=MESH
                )
            )
        return out_copies, in_copies

    out_a, in_a = own_copies(lambda p: send_a.at[p], lambda p: recv_a.at[p], sems_a)
    for copy in out_a:
        copy.start()
    recv_a[g] = send_a[g]

    bincol[...] = jnp.zeros_like(bincol)
    for row in range(G * C):
        bincol[S * row : S * row + S, :] = jnp.full((S, LANES), bins[row].astype(F32))
    scale = 1.0 / math.sqrt(G * C)
    at3[...] = jnp.zeros_like(at3)
    for piece in range(DEPTHS // LANES):
        shape = (KP, LANES)
        depth = lax.broadcasted_iota(jnp.int32, shape, 1) + (piece * LANES - DEPTHS // 2)
        product = bincol[...] * depth.astype(F32)
        turns = product - BINS * jnp.floor(product * (1.0 / BINS))
        turns = jnp.where(turns < 0, turns + BINS, turns)
        turns = jnp.where(turns >= BINS, turns - BINS, turns)
        angles = turns * (2.0 * math.pi / BINS)
        row = lax.broadcasted_iota(jnp.int32, shape, 0)
        is_q = (row & 1) == 0
        real = row < G * SC
        cosine = jnp.where(real, jnp.cos(angles) * scale, 0.0)
        sine = jnp.where(real, jnp.sin(angles) * scale, 0.0)
        for half, value in ((0, jnp.where(is_q, cosine, sine)), (1, jnp.where(is_q, -sine, cosine))):
            lanes = pl.ds(half * DEPTHS + piece * LANES, LANES)
            high, low = split(value)
            at2[0:KP, lanes] = high
            at2[KP : 2 * KP, lanes] = low
            at3[0:KP, lanes] = high.astype(F32)
            at3[KP : 2 * KP, lanes] = low.astype(F32)
            at3[2 * KP : 3 * KP, lanes] = high.astype(F32)
    a3[...] = at3[...].T.astype(BF16)
    x[...] = jnp.zeros_like(x)

    shift = int(math.log2(LANES))

    def permute(cells):
        halves = []
        for h in range(Y // 8):
            pixel = order[8 * h : 8 * h + 8, :]
            col = pixel & (LANES - 1)
            row = lax.shift_right_logical(pixel, shift)
            acc = jnp.zeros((8, LANES), F32)
            for y in range(Y):
                taken = jnp.take_along_axis(cells(y), col, axis=1, mode="promise_in_bounds")
                acc = jnp.where(row == y, taken, acc)
            halves.append(acc)
        return jnp.concatenate(halves, axis=0)

    def gather_dirty(c, carry):
        for s in range(S):
            source = (s * C + c) * Y
            target = pl.ds(pl.multiple_of((c * S + s) * Y, 8), Y)
            slots[target, :] = permute(lambda y: jnp.broadcast_to(dirty[pl.ds(source + y, 1), :], (8, LANES)))
        return carry

    lax.fori_loop(0, C, gather_dirty, 0)
    for k in range(NCH):
        pack(send_d, k, slots)
    out_d, in_d = own_copies(lambda p: send_d.at[p], lambda p: recv_d.at[p], sems_d)
    for copy in out_d:
        copy.start()
    recv_d[g] = send_d[g]

    def project(recv):
        for q in range(G):
            for k in range(NCH):
                for r in range(R):
                    x[q * SC + k * W : q * SC + k * W + W, r * LANES : (r + 1) * LANES] = recv[
                        q, k, r * W : r * W + W, :
                    ]
        high, low = split(x[...])
        parts = [high, high, low]
        if d["K3"] > 3 * KP:
            parts.append(jnp.zeros((d["K3"] - 3 * KP, x.shape[1]), BF16))
        big[...] = mxu(a3[...], jnp.concatenate(parts, axis=0))

    BLOCK = 16

    for copy in in_a:
        copy.wait_recv()
    project(recv_a)

    def shrink_first(i, carry):
        top = pl.ds(pl.multiple_of(i * BLOCK, BLOCK), BLOCK)
        low = pl.ds(pl.multiple_of(DEPTHS + i * BLOCK, BLOCK), BLOCK)
        a, b = shrink_pair(big[top, :], big[low, :])
        first_hi[top, :], first_lo[top, :] = split(a)
        first_hi[low, :], first_lo[low, :] = split(b)
        return carry

    lax.fori_loop(0, DEPTHS // BLOCK, shrink_first, 0)
    both = mxu(at2[...], first_hi[...])
    model[...] = both[:KP] + both[KP:] + mxu(at2[0:KP, :], first_lo[...])

    up = g * R < HALF
    goes = jnp.logical_or(jnp.logical_and(up, has_prev), jnp.logical_and(jnp.logical_not(up), has_next))
    toward = jnp.where(up, before, after)
    copies_m, copies_h = [], []
    for k in range(NCH):
        for p in range(G):
            for r in range(R):
                send_m[p, k, r * W : r * W + W, :] = model[
                    p * SC + k * W : p * SC + k * W + W, r * LANES : (r + 1) * LANES
                ]
        halo = [
            pltpu.make_async_remote_copy(
                send_m.at[p, k],
                recv_h.at[g, k],
                sems_h.at[0, p, k],
                sems_h.at[1, g, k],
                device_id=(p, toward),
                device_id_type=MESH,
            )
            for p in range(G)
        ]
        copies_h.append(halo)

        @pl.when(goes)
        def _():
            for copy in halo:
                copy.start()

        copies = own_copies(
            lambda p: send_m.at[p, k], lambda p: recv_m.at[p, k], sems_m, k
        )
        copies_m.append(copies)
        for copy in copies[0]:
            copy.start()
        recv_m[g, k] = send_m[g, k]

    for copy in in_d:
        copy.wait_recv()
    project(recv_d)

    def shrink_slots(i, carry):
        top = pl.ds(pl.multiple_of(i * BLOCK, BLOCK), BLOCK)
        low = pl.ds(pl.multiple_of(DEPTHS + i * BLOCK, BLOCK), BLOCK)
        first_slots[top, :], first_slots[low, :] = shrink_pair(big[top, :], big[low, :])
        return carry

    lax.fori_loop(0, DEPTHS // BLOCK, shrink_slots, 0)

    PY = Y + 2 * HALF
    lane = lax.broadcasted_iota(jnp.int32, (Y, LANES), 1)
    blocks = [range(0, (BEAM + 1) // 2), range((BEAM + 1) // 2, BEAM)]

    def convolve(c, carry):
        totals = [jnp.zeros((Y, LANES), F32) for _ in range(S)]
        for block in blocks:
            sums = [[None] * len(block) for _ in range(S)]
            for i in range(BEAM):
                rows = [padded[pl.ds((c * S + s) * PY + i, Y), :] for s in range(S)]
                for n, j in enumerate(block):
                    tap = beams[c, i * BEAM + j]
                    for s in range(S):
                        term = tap * rows[s]
                        sums[s][n] = term if i == 0 else sums[s][n] + term
            for n, j in enumerate(block):
                inside = jnp.logical_and(lane + (j - HALF) >= 0, lane + (j - HALF) < LANES)
                for s in range(S):
                    moved = sums[s][n]
                    if j != HALF:
                        moved = pltpu.roll(moved, (HALF - j) % LANES, axis=1)
                        moved = jnp.where(inside, moved, 0.0)
                    totals[s] = totals[s] + moved
        for s in range(S):
            cells = pl.ds(pl.multiple_of((s * C + c) * Y, 8), Y)
            res[cells, :] = dirty[cells, :] - totals[s]
        return carry

    def gather_res(c, carry):
        for s in range(S):
            source = (s * C + c) * Y
            target = pl.ds(pl.multiple_of((c * S + s) * Y, 8), Y)
            slots[target, :] = permute(lambda y: jnp.broadcast_to(res[pl.ds(source + y, 1), :], (8, LANES)))
        return carry

    def halo_block(q, k, ok):
        arrived = pltpu.make_async_remote_copy(
            send_m.at[q, k],
            recv_h.at[q, k],
            sems_h.at[0, q, k],
            sems_h.at[1, q, k],
            device_id=(q, t),
            device_id_type=MESH,
        )

        @pl.when(ok)
        def _():
            arrived.wait_recv()

        @pl.when(jnp.logical_not(ok))
        def _():
            recv_h[q, k] = jnp.zeros(recv_h.shape[2:], F32)

    copies_r = []
    for k in range(NCH):
        for copy in copies_m[k][1]:
            copy.wait_recv()
        for q in range(G):
            from_next = q * R < HALF
            halo_block(q, k, has_next if from_next else has_prev)
            at_row = Y + HALF + q * R if from_next else q * R - HALF
            for r in range(R):
                padded[pl.ds(k * W * PY + HALF + q * R + r, W, stride=PY), :] = recv_m[
                    q, k, r * W : r * W + W, :
                ]
                padded[pl.ds(k * W * PY + at_row + r, W, stride=PY), :] = recv_h[
                    q, k, r * W : r * W + W, :
                ]
        lax.fori_loop(k * CC, (k + 1) * CC, convolve, 0)
        lax.fori_loop(k * CC, (k + 1) * CC, gather_res, 0)
        pack(send_r, k, slots)
        copies = own_copies(
            lambda p: send_r.at[p, k], lambda p: recv_r.at[p, k], sems_r, k
        )
        copies_r.append(copies)
        for copy in copies[0]:
            copy.start()
        recv_r[g, k] = send_r[g, k]

    for k in range(NCH):
        for copy in copies_r[k][1]:
            copy.wait_recv()
    project(recv_r)

    def finish(i, carry, tail=0):
        top = pl.ds(pl.multiple_of(i * BLOCK, BLOCK), BLOCK)
        low = pl.ds(pl.multiple_of(DEPTHS + i * BLOCK, BLOCK), BLOCK)
        a, b = shrink_pair(
            first_slots[top, :] + STEP_SIZE * big[top, :], first_slots[low, :] + STEP_SIZE * big[low, :]
        )
        for start, value in ((0, a), (DEPTHS, b)):
            for r in range(R):
                piece = value[:, r * LANES : (r + 1) * LANES]
                base = (start + i * BLOCK) * R + r
                out[pl.ds(base, BLOCK - tail, stride=R), :] = piece[: BLOCK - tail]
                if tail:
                    out[pl.ds(base + (BLOCK - tail) * R, tail), :] = piece[BLOCK - tail :]
        return carry

    lax.fori_loop(0, DEPTHS // BLOCK - 1, finish, 0)
    finish(DEPTHS // BLOCK - 1, 0, 1)

    for copy in out_a + out_d:
        copy.wait_send()
    for k in range(NCH):
        for copy in copies_m[k][0] + copies_r[k][0]:
            copy.wait_send()

    @pl.when(goes)
    def _():
        for halo in copies_h:
            for copy in halo:
                copy.wait_send()


def on_device(dirty, beams, chan_bins, pixel_order):
    S, C, Y, X = dirty.shape
    G = lax.axis_size("chan")
    T = lax.axis_size("tile")
    BEAM = math.isqrt(beams.shape[1])
    HALF = (BEAM - 1) // 2
    R = Y // G
    CC = 3 if C % 3 == 0 else C
    NCH = C // CC
    W = S * CC
    SC = S * C
    KP = round_up(G * SC, 16)
    K3 = round_up(3 * KP, LANES)
    PB = round_up(R * W, 8)
    N = R * X
    d = dict(G=G, T=T, R=R, Y=Y, C=C, S=S, W=W, CC=CC, NCH=NCH, HALF=HALF, BEAM=BEAM, KP=KP, K3=K3)
    vmem = pl.BlockSpec(memory_space=pltpu.VMEM)
    smem = pl.BlockSpec(memory_space=pltpu.SMEM)
    block = pltpu.VMEM((G, NCH, PB, LANES), F32)
    dma = pltpu.SemaphoreType.DMA
    spectrum, residual = pl.pallas_call(
        functools.partial(kernel, d),
        out_shape=(
            jax.ShapeDtypeStruct((2 * DEPTHS * R, LANES), F32),
            jax.ShapeDtypeStruct((SC * Y, X), F32),
        ),
        in_specs=[vmem, smem, smem, vmem],
        out_specs=(vmem, vmem),
        scratch_shapes=[
            pltpu.VMEM((KP, LANES), F32),
            pltpu.VMEM((K3, 2 * DEPTHS), F32),
            pltpu.VMEM((2 * DEPTHS, K3), BF16),
            pltpu.VMEM((2 * KP, 2 * DEPTHS), BF16),
            pltpu.VMEM((KP, N), F32),
            pltpu.VMEM((2 * DEPTHS, N), F32),
            pltpu.VMEM((2 * DEPTHS, N), BF16),
            pltpu.VMEM((2 * DEPTHS, N), BF16),
            pltpu.VMEM((2 * DEPTHS, N), F32),
            pltpu.VMEM((KP, N), F32),
            pltpu.VMEM(((SC + 1) * (Y + 2 * HALF), LANES), F32),
            pltpu.VMEM(((SC + 1) * Y, LANES), F32),
            pltpu.VMEM(((SC + 1) * Y, LANES), F32),
        ]
        + [block] * 9
        + [dma((2, G)), dma((2, G)), dma((2, G, NCH)), dma((2, G, NCH)), dma((2, G, NCH))],
        compiler_params=pltpu.CompilerParams(
            collective_id=0, has_side_effects=True, vmem_limit_bytes=48 * 1024 * 1024
        ),
    )(dirty.reshape(SC * Y, X), beams, chan_bins, pixel_order.reshape(Y, X))
    return spectrum.reshape(2, DEPTHS, 1, N), residual.reshape(dirty.shape)


def solution(mesh):
    placed = (P(None, "chan", "tile", None), P("chan", None), P(), P("tile", None))
    return jax.shard_map(
        on_device,
        mesh=mesh,
        in_specs=placed,
        out_specs=(P(None, None, "tile", "chan"), P(None, "chan", "tile", None)),
        check_vma=False,
    )
```

time: 192 us -> 28.5 us (0.15)
  local copies, waits for them, and re-layouts: 77.6 us -> 4.62 us
  matrix products: 47 us -> 0 us
  other arithmetic: 39.9 us -> 0 us
  Pallas kernels: 0 us -> 22.9 us
  starting transfers between devices: 13 us -> 0 us
  blocking collectives: 8.08 us -> 0 us
  waiting for transfers between devices: 3.89 us -> 0 us
    conv_general_dilated x1 -> x0, matrix products: 42.8 us -> none  [blur(): lax.conv_general_dilated(stacked, kernel, (1, 1), ((row_pad, row_pad), (b...]
    gather x3 -> x0, local copies, waits for them, and re-layouts: 37.3 us -> none  [the longest x2 28.9 us: to_owners(): jnp.take(cube.reshape(pair_count, chan_local, tile_pix), slot_pixels, axi...]
    select_n x5 -> x0, other arithmetic: 35.7 us -> none  [the longest x2 19.9 us: to_owners(): jnp.take(cube.reshape(pair_count, chan_local, tile_pix), slot_pixels, axi...]
    pallas_call x0 -> x1, Pallas kernels: none -> 22.9 us  [on_device(): pl.pallas_call(functools.partial(kernel, d), out_shape=(jax.ShapeDtypeStr...]
    reshape x11 -> x0, local copies, waits for them, and re-layouts: 10.1 us -> none  [the longest x2 3.86 us: to_owners(): slots = slots.reshape(pair_count, chan_local, groups, owned)]
    all_to_all x1 -> x0, blocking collectives: 8.08 us -> none  [to_owners(): lax.all_to_all(slots, 'chan', split_axis=2, concat_axis=1, tiled=True)]
    scatter x1 -> x0, local copies, waits for them, and re-layouts: 8.05 us -> none  [on_device(): jnp.zeros((tile_pix,), jnp.int32).at[slot_pixels]]
    all_to_all x2 -> x0, starting transfers between devices: 7.62 us -> none  [the longest x1 4.26 us: to_owners(): lax.all_to_all(slots, 'chan', split_axis=2, concat_axis=1, tiled=True)]
  transfers between devices with their start and end apart: 4 -> 0, of which waited for: 1 -> 0; matrix products, arithmetic and copies ran while one was open for 12% -> 0% of each run, Pallas kernels for 0% -> 0%
where the time goes in v1:
time: 28.5 us; the launch traced here: 28.2 us
  Pallas kernels  22.9 us (80%)
  local copies, waits for them, and re-layouts  4.62 us (16%)
  between operations  0.65 us (2%)
    pallas_call x1, Pallas kernels, on_device(): pl.pallas_call(functools.partial(kernel, d), out_shape=(jax.ShapeDtypeStr...  22.9 us
    unnamed x10, local copies, waits for them, and re-layouts  4.62 us

profile of v1, /device:TPU:0, one launch (start us, length us, event | category | flops | bytes accessed | tf_op | source)
XLA Modules:
  0.0 28.2 jit_solution(6182081400039220411)
XLA Ops:
  0.6 0.0 copy-start.3
  0.6 0.6 %copy-done.3 = s32[36]{0:T(128)S(1)} copy-done((s32[36]{0:T(128)S(1)}, s32[36]{0:T(128)}, u32[]{:S(2)}) %copy-start.3) | copy-done | bytes 168
  1.3 0.0 copy-start
  1.3 0.9 %copy-done = f32[2,9,16,128]{3,2,1,0:T(8,128)S(1)} copy-done((f32[2,9,16,128]{3,2,1,0:T(8,128)S(1)}, f32[2,9,16,128]{3,2,1,0:T(8,128)}, u32[]{:S(2)}) %copy-start) | copy-done | bytes 147480
  2.2 0.0 copy-start.1
  2.2 0.7 %copy-done.1 = f32[9,289]{1,0:T(8,128)S(1)} copy-done((f32[9,289]{1,0:T(8,128)S(1)}, f32[9,289]{1,0:T(8,128)}, u32[]{:S(2)}) %copy-start.1) | copy-done | bytes 10428
  2.9 0.0 copy-start.2
  2.9 0.7 %copy-done.2 = s32[1,2048]{1,0:T(1,128)S(1)} copy-done((s32[1,2048]{1,0:T(1,128)S(1)}, s32[1,2048]{1,0:T(1,128)}, u32[]{:S(2)}) %copy-start.2) | copy-done | bytes 8216
  3.6 22.9 %shard_map.59 = (f32[2048,128]{1,0:T(8,128)S(1)}, f32[288,128]{1,0:T(8,128)S(1)}) custom-call(f32[288,128]{1,0:T(8,128)S(1)} %bitcast.5, f32[9,289]{1,0:T(8,128)S(1)} %copy-done.1, s32[36]{0:T(128)S(1)} %copy-done.3, s32[16,128]{1,0:T(8,128)S(1)} %bitcast.7), custom_call_target="tpu_custom_call" | custom-call | tf_op jit(solution)/shard_map/pallas_call | solution.py:409
  26.6 1.0 %copy.9 = f32[2,256,1,512]{3,2,1,0:T(1,128)} copy(f32[2,256,1,512]{3,2,1,0:T(1,128)S(1)} %bitcast.4) | data formatting | bytes 2097152
  27.6 0.7 %copy.10 = f32[2,9,16,128]{3,2,1,0:T(8,128)} copy(f32[2,9,16,128]{3,2,1,0:T(8,128)S(1)} %bitcast.6) | data formatting | bytes 294912
Async XLA Ops:
  0.6 0.7 %copy-start.3 = (s32[36]{0:T(128)S(1)}, s32[36]{0:T(128)}, u32[]{:S(2)}) copy-start(s32[36]{0:T(128)} %bins.1) | copy-start | bytes 436
  1.3 0.9 %copy-start = (f32[2,9,16,128]{3,2,1,0:T(8,128)S(1)}, f32[2,9,16,128]{3,2,1,0:T(8,128)}, u32[]{:S(2)}) copy-start(f32[2,9,16,128]{3,2,1,0:T(8,128)} %param.4) | copy-start | bytes 442372
  2.2 0.7 %copy-start.1 = (f32[9,289]{1,0:T(8,128)S(1)}, f32[9,289]{1,0:T(8,128)}, u32[]{:S(2)}) copy-start(f32[9,289]{1,0:T(8,128)} %beams.1) | copy-start | bytes 31216
  2.9 0.7 %copy-start.2 = (s32[1,2048]{1,0:T(1,128)S(1)}, s32[1,2048]{1,0:T(1,128)}, u32[]{:S(2)}) copy-start(s32[1,2048]{1,0:T(1,128)} %param.7) | copy-start | bytes 24580

commit v2 on v1

--- a/solution.py
+++ b/solution.py
@@ -33,18 +33,26 @@
     return a * factor, b * factor
 
 
+def aligned(row):
+    return row if isinstance(row, int) else pl.multiple_of(row, 8)
+
+
 def mxu(a, b):
     return jnp.dot(a, b, preferred_element_type=F32)
 
 
 def kernel(
     d,
+    dirty_hbm,
+    beams_hbm,
+    bins_hbm,
+    order_hbm,
+    out,
+    res,
     dirty,
     beams,
     bins,
     order,
-    out,
-    res,
     bincol,
     at3,
     a3,
@@ -72,6 +80,7 @@
     sems_m,
     sems_h,
     sems_r,
+    sems_in,
 ):
     G, T, R, Y, C, S, W, CC, NCH, HALF, BEAM = (
         d["G"], d["T"], d["R"], d["Y"], d["C"], d["S"], d["W"], d["CC"], d["NCH"], d["HALF"], d["BEAM"]
@@ -85,6 +94,10 @@
     before = lax.rem(t + T - 1, T)
     after = lax.rem(t + 1, T)
 
+    pairs = ((dirty_hbm, dirty), (bins_hbm, bins), (beams_hbm, beams), (order_hbm, order))
+    loads = [pltpu.make_async_copy(src, dst, sems_in.at[n]) for n, (src, dst) in enumerate(pairs)]
+    for load in loads:
+        load.start()
     barrier = pltpu.get_barrier_semaphore()
     for step in range(1, G):
         pl.semaphore_signal(barrier, inc=1, device_id=(lax.rem(g + step, G), t), device_id_type=MESH)
@@ -104,6 +117,7 @@
             for r in range(R):
                 send[p, k, r * W : r * W + W, :] = cells[pl.ds(k * W * Y + p * R + r, W, stride=Y), :]
 
+    loads[0].wait()
     for c in range(C):
         for s in range(S):
             mixed[(c * S + s) * Y : (c * S + s) * Y + Y, :] = dirty[(s * C + c) * Y : (s * C + c) * Y + Y, :]
@@ -133,6 +147,8 @@
         copy.start()
     recv_a[g] = send_a[g]
 
+    for load in loads[1:]:
+        load.wait()
     bincol[...] = jnp.zeros_like(bincol)
     for row in range(G * C):
         bincol[S * row : S * row + S, :] = jnp.full((S, LANES), bins[row].astype(F32))
@@ -180,17 +196,9 @@
     def gather_dirty(c, carry):
         for s in range(S):
             source = (s * C + c) * Y
-            target = pl.ds(pl.multiple_of((c * S + s) * Y, 8), Y)
+            target = pl.ds(aligned((c * S + s) * Y), Y)
             slots[target, :] = permute(lambda y: jnp.broadcast_to(dirty[pl.ds(source + y, 1), :], (8, LANES)))
         return carry
-
-    lax.fori_loop(0, C, gather_dirty, 0)
-    for k in range(NCH):
-        pack(send_d, k, slots)
-    out_d, in_d = own_copies(lambda p: send_d.at[p], lambda p: recv_d.at[p], sems_d)
-    for copy in out_d:
-        copy.start()
-    recv_d[g] = send_d[g]
 
     def project(recv):
         for q in range(G):
@@ -259,17 +267,13 @@
             copy.start()
         recv_m[g, k] = send_m[g, k]
 
-    for copy in in_d:
-        copy.wait_recv()
-    project(recv_d)
-
-    def shrink_slots(i, carry):
-        top = pl.ds(pl.multiple_of(i * BLOCK, BLOCK), BLOCK)
-        low = pl.ds(pl.multiple_of(DEPTHS + i * BLOCK, BLOCK), BLOCK)
-        first_slots[top, :], first_slots[low, :] = shrink_pair(big[top, :], big[low, :])
-        return carry
-
-    lax.fori_loop(0, DEPTHS // BLOCK, shrink_slots, 0)
+    lax.fori_loop(0, C, gather_dirty, 0)
+    for k in range(NCH):
+        pack(send_d, k, slots)
+    out_d, in_d = own_copies(lambda p: send_d.at[p], lambda p: recv_d.at[p], sems_d)
+    for copy in out_d:
+        copy.start()
+    recv_d[g] = send_d[g]
 
     PY = Y + 2 * HALF
     lane = lax.broadcasted_iota(jnp.int32, (Y, LANES), 1)
@@ -295,14 +299,14 @@
                         moved = jnp.where(inside, moved, 0.0)
                     totals[s] = totals[s] + moved
         for s in range(S):
-            cells = pl.ds(pl.multiple_of((s * C + c) * Y, 8), Y)
+            cells = pl.ds(aligned((s * C + c) * Y), Y)
             res[cells, :] = dirty[cells, :] - totals[s]
         return carry
 
     def gather_res(c, carry):
         for s in range(S):
             source = (s * C + c) * Y
-            target = pl.ds(pl.multiple_of((c * S + s) * Y, 8), Y)
+            target = pl.ds(aligned((c * S + s) * Y), Y)
             slots[target, :] = permute(lambda y: jnp.broadcast_to(res[pl.ds(source + y, 1), :], (8, LANES)))
         return carry
 
@@ -325,6 +329,19 @@
             recv_h[q, k] = jnp.zeros(recv_h.shape[2:], F32)
 
     copies_r = []
+
+    def step(c, carry):
+        gather_res(c - 1, 0)
+        return convolve(c, carry)
+
+    def send_slots(k):
+        pack(send_r, k, slots)
+        copies = own_copies(lambda p: send_r.at[p, k], lambda p: recv_r.at[p, k], sems_r, k)
+        copies_r.append(copies)
+        for copy in copies[0]:
+            copy.start()
+        recv_r[g, k] = send_r[g, k]
+
     for k in range(NCH):
         for copy in copies_m[k][1]:
             copy.wait_recv()
@@ -339,16 +356,26 @@
                 padded[pl.ds(k * W * PY + at_row + r, W, stride=PY), :] = recv_h[
                     q, k, r * W : r * W + W, :
                 ]
-        lax.fori_loop(k * CC, (k + 1) * CC, convolve, 0)
-        lax.fori_loop(k * CC, (k + 1) * CC, gather_res, 0)
-        pack(send_r, k, slots)
-        copies = own_copies(
-            lambda p: send_r.at[p, k], lambda p: recv_r.at[p, k], sems_r, k
-        )
-        copies_r.append(copies)
-        for copy in copies[0]:
-            copy.start()
-        recv_r[g, k] = send_r[g, k]
+        if k == 0:
+            convolve(0, 0)
+        else:
+            step(k * CC, 0)
+            send_slots(k - 1)
+        lax.fori_loop(k * CC + 1, (k + 1) * CC, step, 0)
+    gather_res(C - 1, 0)
+    send_slots(NCH - 1)
+
+    for copy in in_d:
+        copy.wait_recv()
+    project(recv_d)
+
+    def shrink_slots(i, carry):
+        top = pl.ds(pl.multiple_of(i * BLOCK, BLOCK), BLOCK)
+        low = pl.ds(pl.multiple_of(DEPTHS + i * BLOCK, BLOCK), BLOCK)
+        first_slots[top, :], first_slots[low, :] = shrink_pair(big[top, :], big[low, :])
+        return carry
+
+    lax.fori_loop(0, DEPTHS // BLOCK, shrink_slots, 0)
 
     for k in range(NCH):
         for copy in copies_r[k][1]:
@@ -403,7 +430,7 @@
     N = R * X
     d = dict(G=G, T=T, R=R, Y=Y, C=C, S=S, W=W, CC=CC, NCH=NCH, HALF=HALF, BEAM=BEAM, KP=KP, K3=K3)
     vmem = pl.BlockSpec(memory_space=pltpu.VMEM)
-    smem = pl.BlockSpec(memory_space=pltpu.SMEM)
+    hbm = pl.BlockSpec(memory_space=pltpu.HBM)
     block = pltpu.VMEM((G, NCH, PB, LANES), F32)
     dma = pltpu.SemaphoreType.DMA
     spectrum, residual = pl.pallas_call(
@@ -412,9 +439,13 @@
             jax.ShapeDtypeStruct((2 * DEPTHS * R, LANES), F32),
             jax.ShapeDtypeStruct((SC * Y, X), F32),
         ),
-        in_specs=[vmem, smem, smem, vmem],
+        in_specs=[hbm, hbm, hbm, hbm],
         out_specs=(vmem, vmem),
         scratch_shapes=[
+            pltpu.VMEM((SC * Y, X), F32),
+            pltpu.SMEM(beams.shape, F32),
+            pltpu.SMEM(chan_bins.shape, jnp.int32),
+            pltpu.VMEM((Y, X), jnp.int32),
             pltpu.VMEM((KP, LANES), F32),
             pltpu.VMEM((K3, 2 * DEPTHS), F32),
             pltpu.VMEM((2 * DEPTHS, K3), BF16),
@@ -430,7 +461,7 @@
             pltpu.VMEM(((SC + 1) * Y, LANES), F32),
         ]
         + [block] * 9
-        + [dma((2, G)), dma((2, G)), dma((2, G, NCH)), dma((2, G, NCH)), dma((2, G, NCH))],
+        + [dma((2, G)), dma((2, G)), dma((2, G, NCH)), dma((2, G, NCH)), dma((2, G, NCH)), dma((4,))],
         compiler_params=pltpu.CompilerParams(
             collective_id=0, has_side_effects=True, vmem_limit_bytes=48 * 1024 * 1024
         ),

time: 28.5 us -> 26.6 us (0.933)
  Pallas kernels: 22.9 us -> 21.1 us
    pallas_call x1, Pallas kernels: 22.9 us -> 21.1 us  [on_device(): pl.pallas_call(functools.partial(kernel, d), out_shape=(jax.ShapeDtypeStr...]
where the time goes in v2:
time: 26.6 us; the launch traced here: 26.4 us
  Pallas kernels  21.1 us (79%)
  local copies, waits for them, and re-layouts  4.62 us (17%)
  between operations  0.65 us (2%)
    pallas_call x1, Pallas kernels, on_device(): pl.pallas_call(functools.partial(kernel, d), out_shape=(jax.ShapeDtypeStr...  21.1 us
    unnamed x10, local copies, waits for them, and re-layouts  4.62 us

profile of v2, /device:TPU:0, one launch (start us, length us, event | category | flops | bytes accessed | tf_op | source)
XLA Modules:
  0.0 26.4 jit_solution(15352706271693339948)
XLA Ops:
  0.6 0.0 copy-start.3
  0.6 0.6 %copy-done.3 = s32[36]{0:T(128)S(1)} copy-done((s32[36]{0:T(128)S(1)}, s32[36]{0:T(128)}, u32[]{:S(2)}) %copy-start.3) | copy-done | bytes 168
  1.3 0.0 copy-start
  1.3 0.9 %copy-done = f32[2,9,16,128]{3,2,1,0:T(8,128)S(1)} copy-done((f32[2,9,16,128]{3,2,1,0:T(8,128)S(1)}, f32[2,9,16,128]{3,2,1,0:T(8,128)}, u32[]{:S(2)}) %copy-start) | copy-done | bytes 147480
  2.2 0.0 copy-start.1
  2.2 0.7 %copy-done.1 = f32[9,289]{1,0:T(8,128)S(1)} copy-done((f32[9,289]{1,0:T(8,128)S(1)}, f32[9,289]{1,0:T(8,128)}, u32[]{:S(2)}) %copy-start.1) | copy-done | bytes 10428
  2.9 0.0 copy-start.2
  2.9 0.7 %copy-done.2 = s32[1,2048]{1,0:T(1,128)S(1)} copy-done((s32[1,2048]{1,0:T(1,128)S(1)}, s32[1,2048]{1,0:T(1,128)}, u32[]{:S(2)}) %copy-start.2) | copy-done | bytes 8216
  3.6 21.1 %shard_map.59 = (f32[2048,128]{1,0:T(8,128)S(1)}, f32[288,128]{1,0:T(8,128)S(1)}) custom-call(f32[288,128]{1,0:T(8,128)S(1)} %bitcast.5, f32[9,289]{1,0:T(8,128)S(1)} %copy-done.1, s32[36]{0:T(128)S(1)} %copy-done.3, s32[16,128]{1,0:T(8,128)S(1)} %bitcast.7), custom_call_target="tpu_custom_call" | custom-call | tf_op jit(solution)/shard_map/pallas_call | solution.py:436
  24.7 1.0 %copy.9 = f32[2,256,1,512]{3,2,1,0:T(1,128)} copy(f32[2,256,1,512]{3,2,1,0:T(1,128)S(1)} %bitcast.4) | data formatting | bytes 2097152
  25.7 0.7 %copy.10 = f32[2,9,16,128]{3,2,1,0:T(8,128)} copy(f32[2,9,16,128]{3,2,1,0:T(8,128)S(1)} %bitcast.6) | data formatting | bytes 294912
Async XLA Ops:
  0.6 0.7 %copy-start.3 = (s32[36]{0:T(128)S(1)}, s32[36]{0:T(128)}, u32[]{:S(2)}) copy-start(s32[36]{0:T(128)} %bins_hbm.1) | copy-start | bytes 436
  1.3 0.9 %copy-start = (f32[2,9,16,128]{3,2,1,0:T(8,128)S(1)}, f32[2,9,16,128]{3,2,1,0:T(8,128)}, u32[]{:S(2)}) copy-start(f32[2,9,16,128]{3,2,1,0:T(8,128)} %param.4) | copy-start | bytes 442372
  2.2 0.7 %copy-start.1 = (f32[9,289]{1,0:T(8,128)S(1)}, f32[9,289]{1,0:T(8,128)}, u32[]{:S(2)}) copy-start(f32[9,289]{1,0:T(8,128)} %beams_hbm.1) | copy-start | bytes 31216
  2.9 0.7 %copy-start.2 = (s32[1,2048]{1,0:T(1,128)S(1)}, s32[1,2048]{1,0:T(1,128)}, u32[]{:S(2)}) copy-start(s32[1,2048]{1,0:T(1,128)} %param.7) | copy-start | bytes 24580

commit v3 on v2

--- a/solution.py
+++ b/solution.py
@@ -433,6 +433,7 @@
     hbm = pl.BlockSpec(memory_space=pltpu.HBM)
     block = pltpu.VMEM((G, NCH, PB, LANES), F32)
     dma = pltpu.SemaphoreType.DMA
+    args = (dirty.reshape(SC * Y, X), beams, chan_bins, pixel_order.reshape(Y, X))
     spectrum, residual = pl.pallas_call(
         functools.partial(kernel, d),
         out_shape=(
@@ -465,7 +466,7 @@
         compiler_params=pltpu.CompilerParams(
             collective_id=0, has_side_effects=True, vmem_limit_bytes=48 * 1024 * 1024
         ),
-    )(dirty.reshape(SC * Y, X), beams, chan_bins, pixel_order.reshape(Y, X))
+    )(*(pltpu.with_memory_space_constraint(arg, pltpu.HBM) for arg in args))
     return spectrum.reshape(2, DEPTHS, 1, N), residual.reshape(dirty.shape)
 
 

time: 26.6 us -> 23.3 us (0.88)
  local copies, waits for them, and re-layouts: 4.62 us -> 1.63 us
    unnamed x10 -> x2, local copies, waits for them, and re-layouts: 4.62 us -> 1.63 us
where the time goes in v3:
time: 23.3 us; the launch traced here: 23.2 us
  Pallas kernels  20.9 us (90%)
  local copies, waits for them, and re-layouts  1.63 us (7%)
  between operations  0.64 us (3%)
    pallas_call x1, Pallas kernels, on_device(): pl.pallas_call(functools.partial(kernel, d), out_shape=(jax.ShapeDtypeStr...  20.9 us
    unnamed x2, local copies, waits for them, and re-layouts  1.63 us

profile of v3, /device:TPU:0, one launch (start us, length us, event | category | flops | bytes accessed | tf_op | source)
XLA Modules:
  0.0 23.2 jit_solution(13745320788273117066)
XLA Ops:
  0.6 20.9 %shard_map.59 = (f32[2048,128]{1,0:T(8,128)S(1)}, f32[288,128]{1,0:T(8,128)S(1)}) custom-call(f32[288,128]{1,0:T(8,128)} %bitcast.6, f32[9,289]{1,0:T(8,128)} %beams_hbm.1, s32[36]{0:T(128)} %bins_hbm.1, s32[16,128]{1,0:T(8,128)} %bitcast.7), custom_call_target="tpu_custom_call" | custom-call | tf_op jit(solution)/shard_map/pallas_call | solution.py:437
  21.6 1.0 %copy.9 = f32[2,256,1,512]{3,2,1,0:T(1,128)} copy(f32[2,256,1,512]{3,2,1,0:T(1,128)S(1)} %bitcast.4) | data formatting | bytes 2097152
  22.5 0.7 %copy.10 = f32[2,9,16,128]{3,2,1,0:T(8,128)} copy(f32[2,9,16,128]{3,2,1,0:T(8,128)S(1)} %bitcast.5) | data formatting | bytes 294912
